TPU v7x, 768 devices: a whole 4x8x12 slice. The times are simulated.
768 devices in a mesh: slab: 192 (over z, y_hi, x, core), dom: 4 (over y_lo).
Axes of the slice: x: 4, y: 8 (y_hi: 2, y_lo: 4; y = y_hi * 4 + y_lo), z: 12, core: 2. Of those that a mesh axis runs over, the one named last changes fastest.
Arguments:
- positions: float32 [3, 4718592], P(None, ('slab', 'dom')), may hold values from -6 to 6
- velocities: float32 [3, 4718592], P(None, ('slab', 'dom')), may hold values from -6 to 6
- masses: float32 [4718592], P(('slab', 'dom')), may hold values from 0.2 to 2
- owner_cell: int32 [4718592, 1], P(('slab', 'dom')), may hold values from 0 to 255; in each aligned block of 6144 rows (0 to 6143, 6144 to 12287, ...) at most 32 rows name the same one
- counts: int32 [768], P(('slab', 'dom')), may hold values from 3072 to 6144, as said below
Outputs:
- state: float32 [10, 192, 256, 128], P(None, 'slab', 'dom')
- buddy: float32 [10, 192, 256, 128], P(None, 'slab', 'dom')
Inputs may be any that keep to these rules, and one draw needn't show every extreme that they name: owner_cell is the partner index of the owner times 64 plus its cell; among the rows of one device no value appears more than 32 times, and some device's rows name one value exactly 32 times. `counts`: some device has all 6144 rows live.
All inputs are finite; a program needn't handle non-finite values.
Results may differ from a plain program's by a relative error of at most 0.0003.
Values sent between devices are 32-bit elements; how exact they have to be, the bound alone decides.
A program may use at most 32 MiB of HBM per device.

v0:
```python
import jax
import jax.numpy as jnp
from jax import lax
from jax.sharding import PartitionSpec as P

CELLS = 64


drift_step = 0.5
kick_step = 0.5
soften = 0.25
reach = 4.0
coupling = 0.25


def with_halo(cells, sides, width):
    for axis, dim in sides:
        count = lax.axis_size(axis)
        head = lax.slice_in_dim(cells, 0, width, axis=dim)
        tail = lax.slice_in_dim(cells, cells.shape[dim] - width, cells.shape[dim], axis=dim)
        cells = jnp.concatenate(
            [
                lax.ppermute(tail, axis, [(i, (i + 1) % count) for i in range(count)]),
                cells,
                lax.ppermute(head, axis, [((i + 1) % count, i) for i in range(count)]),
            ],
            axis=dim,
        )
    return cells


def passed_along(value, axis, by):
    size = lax.axis_size(axis)
    return lax.ppermute(value, axis, [(i, (i + by) % size) for i in range(size)])


def pair_accel(centre, others):
    separation = others[:3, None, :] - centre[:3, :, None]
    distance = jnp.sum(separation * separation, axis=0)
    inverse = lax.rsqrt(distance + soften)
    weight = others[3][None, :] * jnp.exp(-distance / reach) * inverse * inverse * inverse
    return coupling * jnp.sum(weight[None] * separation, axis=2)


def forces(shells, extended):
    width = shells.shape[2]
    centres = shells[:, 0].transpose(1, 0, 2)
    views = jnp.stack([extended[:, :, column : column + width] for column in range(3)], axis=2)
    others = views.transpose(3, 0, 1, 2, 4).reshape(width, 4, 9 * 128)

    def per_cell(pieces):
        return pair_accel(pieces[0], pieces[1])

    result = lax.map(per_cell, (centres, others), batch_size=2)
    return result.transpose(1, 0, 2)[:, None]


def per_device(positions, velocities, masses, owner_cell, counts):
    rows_dev = positions.shape[1]
    n_dom = lax.axis_size("dom")
    lanes = 128 // n_dom
    half_way = lax.axis_size("slab") // 2
    moved = positions + drift_step * velocities
    payload = jnp.concatenate([moved, masses[None, :], velocities], axis=0)
    target = owner_cell[:, 0]
    active = jnp.arange(rows_dev, dtype=jnp.int32) < counts[0]
    targets = n_dom * CELLS
    hits = (
        (target[:, None] == jnp.arange(targets, dtype=jnp.int32)[None, :]) & active[:, None]
    ).astype(jnp.int32)
    ranking = jnp.sum(jnp.cumsum(hits, axis=0) * hits, axis=1) - 1
    dom_target = target // CELLS
    cell_id = target % CELLS
    place = jnp.where(active, (cell_id * n_dom + dom_target) * lanes + ranking, CELLS * 128)
    buffer = jnp.zeros((7, CELLS * 128), jnp.float32).at[:, place].set(payload, mode="drop")
    buffer = buffer.reshape(7, CELLS, n_dom, lanes)
    arrived = lax.all_to_all(buffer, "dom", split_axis=2, concat_axis=2, tiled=True).reshape(
        7, 1, CELLS, 128
    )
    shells = arrived[:4]
    extended = with_halo(shells, (("slab", 1), ("dom", 2)), 1)
    accel = forces(shells, extended)
    occupied = (arrived[3:4] > 0).astype(jnp.float32)
    accel = accel * occupied
    state = jnp.concatenate([arrived[:4], arrived[4:7] + kick_step * accel, accel], axis=0)
    buddy = passed_along(state, "slab", half_way)
    return (state, buddy)


def solution(mesh):
    placed = (
        P(None, ("slab", "dom")),
        P(None, ("slab", "dom")),
        P(("slab", "dom")),
        P(("slab", "dom"), None),
        P(("slab", "dom")),
    )
    return jax.shard_map(
        per_device,
        mesh=mesh,
        in_specs=placed,
        out_specs=(P(None, "slab", "dom", None), P(None, "slab", "dom", None)),
        check_vma=False,
    )
```

profile of v0, /device:TPU:63, one launch (start us, length us, event | category | flops | bytes accessed | tf_op | source)
XLA Modules:
  0.0 175.7 jit_solution(2399012052813108706)
XLA Ops:
  1.3 0.8 copy.84
  2.1 1.7 fusion.3
  3.8 2.7 %copy-done = s32[256,48,128]{0,1,2:T(8,128)} copy-done((s32[256,48,128]{0,1,2:T(8,128)}, s32[256,48,128]{0,1,2:T(8,128)S(1)}, u32[]{:S(2)}) %copy-start) | copy-done | bytes 6291480
  6.6 3.4 %broadcast_add_fusion = s32[256,48,128]{0,1,2:T(8,128)S(1)} fusion(s32[256,48,128]{0,1,2:T(8,128)} %copy-done, s32[256,48]{0,1:T(8,128)S(1)} %slice.61), kind=kLoop, calls=%fused_computation.20 | loop fusion | flops 1572864 | bytes 12632064 | tf_op jit(solution)/shard_map/reduce_window_sum
  10.0 3.6 %copy.85 = s32[256,48,128]{0,2,1:T(8,128)S(1)} copy(s32[256,48,128]{0,1,2:T(8,128)S(1)} %broadcast_add_fusion) | data formatting | bytes 12582912 | tf_op jit(solution)/shard_map/reduce_window_sum
  13.8 5.2 %fusion.2 = s32[6144]{0:T(1024)S(1)} fusion(s32[256,48,128]{0,2,1:T(8,128)S(1)} %copy.85, s32[6144]{0:T(1024)S(1)} %bitcast.89, pred[6144]{0:T(1024)(128)(4,1)S(1)} %iota_compare_fusion.2), kind=kLoop, calls=%fused_computation.13 | loop fusion | flops 6285312 | bytes 6346752 | tf_op jit(solution)/shard_map/reduce_sum | solution.py:71
  19.1 1.1 copy.86
  20.5 17.8 %scatter_custom_fusion = f32[7,8192]{0,1:T(8,128)} fusion(s32[6144]{0:T(1024)S(1)} %bitcast.94, f32[6144,7]{1,0:T(8,128)S(1)} %copy.86, f32[]{:T(128)} %constant.58.clone.1), kind=kCustom, calls=%fused_computation.24 | custom fusion | bytes 229380 | tf_op jit(solution)/shard_map/scatter | solution.py:75
  38.2 3.8 %copy.87 = f32[7,64,4,32]{1,3,0,2:T(8,128)S(1)} copy(f32[7,64,4,32]{0,3,2,1:T(8,128)} %bitcast.71) | data formatting | bytes 458752 | tf_op jit(solution)/shard_map/reshape | solution.py:76
  42.3 11.1 %all_to_all.5 = f32[4,1,14336]{2,1,0:T(1,128)S(1)} all-to-all(f32[4,1,14336]{2,1,0:T(1,128)S(1)} %reshape.114), channel_id=1, replica_groups=mesh['slab'=192,'dom'=4] {'dom'}, dimensions={0} | all-to-all | bytes 458752 | tf_op jit(solution)/shard_map/all_to_all | solution.py:77
  53.4 0.5 broadcast.124
  53.9 1.3 reduce
  55.5 6.4 %collective-permute-start = (f32[4,1,64,128]{2,3,0,1:T(8,128)S(1)}, f32[4,1,64,128]{2,3,0,1:T(8,128)S(1)}, u32[]{:S(2)}, u32[]{:S(2)}) collective-permute-start(f32[4,1,64,128]{2,3,0,1:T(8,128)S(1)} %bitcast.72), channel_id=1, source_target_pairs={{0,4},{4,8},{8,12},{12,16},{16,20},{20,24},{24,28},{28,32},{32,36}... | collective-permute-start | bytes 393224 | tf_op jit(solution)/shard_map/ppermute | solution.py:23
  61.9 1.9 %collective-permute-start.1 = (f32[4,1,64,128]{2,3,0,1:T(8,128)S(1)}, f32[4,1,64,128]{2,3,0,1:T(8,128)S(1)}, u32[]{:S(2)}, u32[]{:S(2)}) collective-permute-start(f32[4,1,64,128]{2,3,0,1:T(8,128)S(1)} %bitcast.73), channel_id=1, source_target_pairs={{4,0},{8,4},{12,8},{16,12},{20,16},{24,20},{28,24},{32,28},{36,32}... | collective-permute-start | bytes 393224 | tf_op jit(solution)/shard_map/ppermute | solution.py:25
  63.8 2.1 %collective-permute-done = f32[4,1,64,128]{2,3,0,1:T(8,128)S(1)} collective-permute-done((f32[4,1,64,128]{2,3,0,1:T(8,128)S(1)}, f32[4,1,64,128]{2,3,0,1:T(8,128)S(1)}, u32[]{:S(2)}, u32[]{:S(2)}) %collective-permute-start) | collective-permute-done | bytes 131104 | tf_op jit(solution)/shard_map/ppermute | solution.py:23
  65.9 12.4 %collective-permute-done.1 = f32[4,1,64,128]{2,3,0,1:T(8,128)S(1)} collective-permute-done((f32[4,1,64,128]{2,3,0,1:T(8,128)S(1)}, f32[4,1,64,128]{2,3,0,1:T(8,128)S(1)}, u32[]{:S(2)}, u32[]{:S(2)}) %collective-permute-start.1) | collective-permute-done | bytes 131104 | tf_op jit(solution)/shard_map/ppermute | solution.py:25
  78.9 3.5 %collective-permute-start.2 = (f32[4,3,1,128]{3,0,2,1:T(4,128)S(1)}, f32[4,3,1,128]{3,0,2,1:T(4,128)S(1)}, u32[]{:S(2)}, u32[]{:S(2)}) collective-permute-start(f32[4,3,1,128]{3,0,2,1:T(4,128)S(1)} %copy.90), channel_id=1, source_target_pairs={{0,1},{1,2},{2,3},{3,0},{4,5},{5,6},{6,7},{7,4},{8,9},{9,10},{10,1... | collective-permute-start | bytes 18440 | tf_op jit(solution)/shard_map/ppermute | solution.py:23
  82.6 1.9 %collective-permute-start.3 = (f32[4,3,1,128]{3,0,2,1:T(4,128)S(1)}, f32[4,3,1,128]{3,0,2,1:T(4,128)S(1)}, u32[]{:S(2)}, u32[]{:S(2)}) collective-permute-start(f32[4,3,1,128]{3,0,2,1:T(4,128)S(1)} %copy.92), channel_id=1, source_target_pairs={{1,0},{2,1},{3,2},{0,3},{5,4},{6,5},{7,6},{4,7},{9,8},{10,9},{11,1... | collective-permute-start | bytes 18440 | tf_op jit(solution)/shard_map/ppermute | solution.py:25
  85.0 3.8 %collective-permute-done.3 = f32[4,3,1,128]{3,0,2,1:T(4,128)S(1)} collective-permute-done((f32[4,3,1,128]{3,0,2,1:T(4,128)S(1)}, f32[4,3,1,128]{3,0,2,1:T(4,128)S(1)}, u32[]{:S(2)}, u32[]{:S(2)}) %collective-permute-start.3) | collective-permute-done | bytes 6176 | tf_op jit(solution)/shard_map/ppermute | solution.py:25
  89.1 0.7 fusion.13
  90.0 2.0 %copy.94 = f32[64,4,3,3,128]{4,3,2,1,0:T(4,128)} copy(f32[64,4,3,3,128]{0,4,1,2,3:T(8,128)S(1)} %maximum_bitcast_fusion) | data formatting | bytes 2359296 | tf_op jit(solution)/shard_map/transpose | solution.py:49
  92.0 2.4 %reshape_reshape.3 = f32[32,2,4,1152]{3,2,1,0:T(4,128)S(1)} reshape(f32[64,4,3,3,128]{4,3,2,1,0:T(4,128)} %copy.94) | data formatting | bytes 2359296 | tf_op jit(solution)/shard_map/reshape;reshape | solution.py:54
  94.4 47.4 %while.10 = (s32[]{:T(128)}, f32[32,2,3,128]{3,2,1,0:T(4,128)S(1)}, f32[32,2,4,1152]{3,2,1,0:T(4,128)S(1)}, f32[32,2,4,128]{3,1,0,2:T(2,128)S(1)}, s32[]{:T(128)}) while((s32[]{:T(128)}, f32[32,2,3,128]{3,2,1,0:T(4,128)S(1)}, f32[32,2,4,1152]{3,2,1,0:T(4,128)S(1)}, f32[32,2,4,128]{3,1,0,2:T(2,128)S(1)}, s32[]{:T(128)}) %tuple.39), condition=%wide.region_7.8_spmd, body=%wide.region_4.7_spmd.sunk | while | flops 7077890 | bytes 5093449 | solution.py:54
  95.4 0.5 fusion.24
  96.8 0.5 fusion.24
  98.3 0.5 fusion.24
  99.8 0.5 fusion.24
  101.3 0.5 fusion.24
  102.8 0.5 fusion.24
  142.3 15.0 %collective-permute-start.4 = (f32[10,1,64,128]{3,2,1,0:T(8,128)S(1)}, f32[10,1,64,128]{3,2,1,0:T(8,128)S(1)}, u32[]{:S(2)}, u32[]{:S(2)}) collective-permute-start(f32[10,1,64,128]{3,2,1,0:T(8,128)S(1)} %copy.102), channel_id=1, source_target_pairs={{0,384},{4,388},{8,392},{12,396},{16,400},{20,404},{24,408},{28,41... | collective-permute-start | bytes 983048 | tf_op jit(solution)/shard_map/ppermute | solution.py:34
  157.2 17.8 %collective-permute-done.4 = f32[10,1,64,128]{3,2,1,0:T(8,128)S(1)} collective-permute-done((f32[10,1,64,128]{3,2,1,0:T(8,128)S(1)}, f32[10,1,64,128]{3,2,1,0:T(8,128)S(1)}, u32[]{:S(2)}, u32[]{:S(2)}) %collective-permute-start.4) | collective-permute-done | bytes 327712 | tf_op jit(solution)/shard_map/ppermute | solution.py:34
  175.0 0.7 copy.128
  (388 shorter events, 44.9 us)
Async XLA Ops:
  3.8 2.7 %copy-start = (s32[256,48,128]{0,1,2:T(8,128)}, s32[256,48,128]{0,1,2:T(8,128)S(1)}, u32[]{:S(2)}) copy-start(s32[256,48,128]{0,1,2:T(8,128)S(1)} %fusion.3) | copy-start | bytes 18874372
  10.0 3.7 %copy-start.3 = (s32[6144,1]{0,1:T(1,128)S(1)}, s32[6144,1]{0,1:T(1,128)}, u32[]{:S(2)}) copy-start(s32[6144,1]{0,1:T(1,128)} %param.10) | copy-start | bytes 73732
  13.7 5.3 %copy-start.1 = (f32[3,6144]{1,0:T(4,128)S(1)}, f32[3,6144]{1,0:T(4,128)}, u32[]{:S(2)}) copy-start(f32[3,6144]{1,0:T(4,128)} %param.8) | copy-start | bytes 221188
  13.7 5.3 %copy-start.4 = (f32[3,6144]{1,0:T(4,128)S(1)}, f32[3,6144]{1,0:T(4,128)}, u32[]{:S(2)}) copy-start(f32[3,6144]{1,0:T(4,128)} %param.7) | copy-start | bytes 221188
  13.7 5.3 %copy-start.5 = (f32[6144]{0:T(1024)S(1)}, f32[6144]{0:T(1024)}, u32[]{:S(2)}) copy-start(f32[6144]{0:T(1024)} %param.9) | copy-start | bytes 73732
  55.5 10.4 %collective-permute-start = (f32[4,1,64,128]{2,3,0,1:T(8,128)S(1)}, f32[4,1,64,128]{2,3,0,1:T(8,128)S(1)}, u32[]{:S(2)}, u32[]{:S(2)}) collective-permute-start(f32[4,1,64,128]{2,3,0,1:T(8,128)S(1)} %bitcast.72), channel_id=1, source_target_pairs={{0,4},{4,8},{8,12},{12,16},{16,20},{20,24},{24,28},{28,32},{32,36}... | collective-permute-start | bytes 393224 | tf_op jit(solution)/shard_map/ppermute | solution.py:23
  61.9 16.4 %collective-permute-start.1 = (f32[4,1,64,128]{2,3,0,1:T(8,128)S(1)}, f32[4,1,64,128]{2,3,0,1:T(8,128)S(1)}, u32[]{:S(2)}, u32[]{:S(2)}) collective-permute-start(f32[4,1,64,128]{2,3,0,1:T(8,128)S(1)} %bitcast.73), channel_id=1, source_target_pairs={{4,0},{8,4},{12,8},{16,12},{20,16},{24,20},{28,24},{32,28},{36,32}... | collective-permute-start | bytes 393224 | tf_op jit(solution)/shard_map/ppermute | solution.py:25
  78.9 5.9 %collective-permute-start.2 = (f32[4,3,1,128]{3,0,2,1:T(4,128)S(1)}, f32[4,3,1,128]{3,0,2,1:T(4,128)S(1)}, u32[]{:S(2)}, u32[]{:S(2)}) collective-permute-start(f32[4,3,1,128]{3,0,2,1:T(4,128)S(1)} %copy.90), channel_id=1, source_target_pairs={{0,1},{1,2},{2,3},{3,0},{4,5},{5,6},{6,7},{7,4},{8,9},{9,10},{10,1... | collective-permute-start | bytes 18440 | tf_op jit(solution)/shard_map/ppermute | solution.py:23
  82.6 6.2 %collective-permute-start.3 = (f32[4,3,1,128]{3,0,2,1:T(4,128)S(1)}, f32[4,3,1,128]{3,0,2,1:T(4,128)S(1)}, u32[]{:S(2)}, u32[]{:S(2)}) collective-permute-start(f32[4,3,1,128]{3,0,2,1:T(4,128)S(1)} %copy.92), channel_id=1, source_target_pairs={{1,0},{2,1},{3,2},{0,3},{5,4},{6,5},{7,6},{4,7},{9,8},{10,9},{11,1... | collective-permute-start | bytes 18440 | tf_op jit(solution)/shard_map/ppermute | solution.py:25
  142.3 33.5 %copy-start.2 = (f32[10,1,64,128]{3,2,1,0:T(8,128)}, f32[10,1,64,128]{3,2,1,0:T(8,128)S(1)}, u32[]{:S(2)}) copy-start(f32[10,1,64,128]{3,2,1,0:T(8,128)S(1)} %copy.102) | copy-start | bytes 983044
  142.3 32.7 %collective-permute-start.4 = (f32[10,1,64,128]{3,2,1,0:T(8,128)S(1)}, f32[10,1,64,128]{3,2,1,0:T(8,128)S(1)}, u32[]{:S(2)}, u32[]{:S(2)}) collective-permute-start(f32[10,1,64,128]{3,2,1,0:T(8,128)S(1)} %copy.102), channel_id=1, source_target_pairs={{0,384},{4,388},{8,392},{12,396},{16,400},{20,404},{24,408},{28,41... | collective-permute-start | bytes 983048 | tf_op jit(solution)/shard_map/ppermute | solution.py:34
where the time goes:
time: 176 us
  other arithmetic  55.7 us (32%)
  local copies, waits for them, and re-layouts  40 us (23%)
  waiting for transfers between devices  36 us (20%)
  starting transfers between devices  28.6 us (16%)
  blocking collectives  11.1 us (6%)
  loops' own time  2.71 us (2%)
    scatter x1, local copies, waits for them, and re-layouts, per_device(): jnp.zeros((7, CELLS * 128), jnp.float32).at[:, place]  17.8 us
    ppermute x1, waiting for transfers between devices, passed_along(): lax.ppermute(value, axis, [(i, (i + by) % size) for i in range(size)])  17.8 us
    reduce_sum x32, other arithmetic, pair_accel(): return coupling * jnp.sum(weight[None] * separation, axis=2)  16.3 us
    ppermute x2, waiting for transfers between devices, with_halo(): lax.ppermute(head, axis, [((i + 1) % count, i) for i in range(count)])  16.1 us
    ppermute x1, starting transfers between devices, passed_along(): lax.ppermute(value, axis, [(i, (i + by) % size) for i in range(size)])  15 us
    reduce_sum x32, other arithmetic, pair_accel(): distance = jnp.sum(separation * separation, axis=0)  13.1 us
    mul x32, other arithmetic, pair_accel(): others[3][None, :] * jnp.exp(-distance / reach) * inverse * inverse  12.8 us
    all_to_all x1, blocking collectives, per_device(): lax.all_to_all(buffer, 'dom', split_axis=2, concat_axis=2, tiled=True)  11.1 us
  transfers between devices with their start and end apart: 5, of which 4 were waited for; matrix products, arithmetic and copies ran while one was open for 0% of the time, Pallas kernels for 0%

commit v1 on v0

v1 whole, which is shorter than its diff:
```python
import functools
import math

import jax
import jax.numpy as jnp
from jax import lax
from jax.experimental import pallas as pl
from jax.experimental.pallas import tpu as pltpu
from jax.sharding import PartitionSpec as P

CELLS = 64
TILE = 128
SLOT = 32
BLOCK = 256
GROUP = 4
PARTS = 3
UNROLL = 8
F32, BF16 = jnp.float32, jnp.bfloat16
MESH = pl.DeviceIdType.MESH

drift_step = 0.5
kick_step = 0.5
soften = 0.25
reach = 4.0
coupling = 0.25
KAP = math.sqrt(math.log2(math.e) / reach)
C0 = KAP * KAP * soften
SCALE = coupling * 2.0**C0 * KAP**2


def rounded(x):
    return x.astype(BF16).astype(F32)


def place_rows(pos_ref, vel_ref, mass_ref, own_ref, cnt_ref, a_ref, b_ref, d_ref):
    rows = pos_ref.shape[1]
    before = lax.broadcasted_iota(jnp.int32, (BLOCK, BLOCK), 0) < lax.broadcasted_iota(jnp.int32, (BLOCK, BLOCK), 1)
    tri = jnp.concatenate([before.astype(BF16), jnp.ones((BLOCK, 128), BF16)], axis=1)
    owner = lax.broadcasted_iota(jnp.int32, (256, BLOCK), 0)
    ranks = lax.broadcasted_iota(jnp.int32, (SLOT, BLOCK), 0).astype(F32)
    lane = lax.broadcasted_iota(jnp.int32, (1, BLOCK), 1)
    live = cnt_ref[0]
    d_ref[...] = jnp.zeros_like(d_ref)

    def group(g, prefix):
        for q in range(GROUP):
            off = pl.multiple_of((g * GROUP + q) * BLOCK, BLOCK)
            here = pl.ds(q * BLOCK, BLOCK)
            hot = owner == jnp.where(lane + off < live, own_ref[:, pl.ds(off, BLOCK)], -1)
            hot16 = jnp.where(hot, 1.0, 0.0).astype(BF16)
            b_ref[:, here] = hot16
            seen = jnp.dot(hot16, tri, preferred_element_type=F32)
            earlier = seen[:, :BLOCK] + jnp.concatenate([prefix, prefix], axis=1)
            prefix = prefix + seen[:, BLOCK:]
            rank = ranks == jnp.sum(jnp.where(hot, earlier, 0.0), axis=0, keepdims=True)
            v = vel_ref[:, pl.ds(off, BLOCK)]
            x = pos_ref[:, pl.ds(off, BLOCK)] + drift_step * v
            values = [x[0:1], x[1:2], x[2:3], mass_ref[:, pl.ds(off, BLOCK)], v[0:1], v[1:2], v[2:3]]
            for c, value in enumerate(values):
                for piece in range(PARTS):
                    head = rounded(value)
                    a_ref[pl.ds((piece * 7 + c) * SLOT, SLOT), here] = jnp.where(rank, head, 0.0).astype(BF16)
                    value = value - head
        d_ref[...] += lax.dot_general(a_ref[...], b_ref[...], (((1,), (1,)), ((), ())), preferred_element_type=F32)
        return prefix

    lax.fori_loop(0, rows // (GROUP * BLOCK), group, jnp.zeros((256, 128), F32))


def kernel(
    n_slab, n_dom,
    pos_ref, vel_ref, mass_ref, own_ref, cnt_ref, state_ref, buddy_ref,
    a_ref, b_ref, d_ref, sent_ref, got_ref, x_ref, edge_out, edge_in, v_ref, ac_ref, bx_ref, bv_ref, ba_ref,
    xi_ref, j_ref, w_ref, tt_ref, je_ref, we_ref, te_ref, acc_ref, lb_ref,
    route_s, route_r, halo_s, halo_r, edge_s, edge_r, early_s, early_r, late_s, late_r,
):
    s, p = lax.axis_index("slab"), lax.axis_index("dom")
    up, down = lax.rem(s + 1, n_slab), lax.rem(s + n_slab - 1, n_slab)
    right, left = lax.rem(p + 1, n_dom), lax.rem(p + n_dom - 1, n_dom)
    other = lax.rem(s + n_slab // 2, n_slab)

    barrier = pltpu.get_barrier_semaphore()
    peers = [(s, lax.rem(p + t, n_dom)) for t in range(1, n_dom)]
    peers += [(a, b) for a in (up, down) for b in (p, left, right)]
    peers += [(other, p)]
    for peer in peers:
        pl.semaphore_signal(barrier, inc=1, device_id=peer, device_id_type=MESH)

    place_rows(pos_ref, vel_ref, mass_ref, own_ref, cnt_ref, a_ref, b_ref, d_ref)
    placed = d_ref[0:224]
    for piece in range(1, PARTS):
        placed = placed + d_ref[piece * 224 : piece * 224 + 224]
    for half in range(2):
        cols = slice(half * 128, half * 128 + 128)
        first = placed[0:128, cols].T
        second = jnp.concatenate([placed[128:224, cols], jnp.zeros((32, 128), F32)], axis=0).T
        sent_ref[0, cols] = pltpu.roll(first, p * SLOT, 1)
        sent_ref[1, cols] = pltpu.roll(second, p * SLOT, 1)

    pl.semaphore_wait(barrier, len(peers))

    def remote(src, dst, send, recv, device):
        return pltpu.make_async_remote_copy(
            src_ref=src, dst_ref=dst, send_sem=send, recv_sem=recv, device_id=device, device_id_type=MESH
        )

    route = [[], []]
    for half in range(2):
        for t in range(1, n_dom):
            q = lax.rem(p + t, n_dom)
            copy = remote(
                sent_ref.at[half, pl.ds(pl.multiple_of(q * CELLS, CELLS), CELLS)], got_ref.at[half, t - 1],
                route_s.at[half, t - 1], route_r.at[half, t - 1], (s, q),
            )
            copy.start()
            route[half].append(copy)

    acc_ref[...] = jnp.zeros_like(acc_ref)
    xi_ref[...] = jnp.full(xi_ref.shape, C0, F32)
    xi_ref[4] = jnp.zeros(xi_ref.shape[1:], F32)
    edge_out[...] = jnp.zeros_like(edge_out)
    je_ref[...] = jnp.zeros_like(je_ref)
    lane_group = lax.broadcasted_iota(jnp.int32, (CELLS, TILE), 1) // SLOT

    def merged(half, count):
        pieces = [(p, sent_ref[half, pl.ds(pl.multiple_of(p * CELLS, CELLS), CELLS)])]
        for t in range(1, n_dom):
            route[half][t - 1].wait_recv()
            pieces.append((lax.rem(p + n_dom - t, n_dom), got_ref[half, t - 1]))
        out = []
        for c in range(count):
            full = jnp.zeros((CELLS, TILE), F32)
            for source, piece in pieces:
                full = jnp.where(lane_group == lax.rem(source + c, n_dom), piece, full)
            out.append(full if c == 0 else pltpu.roll(full, TILE - c * SLOT, 1))
        return out

    own = merged(0, 4)
    for c in range(4):
        x_ref[0, c] = own[c]
        edge_out[0, c : c + 1] = own[c][0:1]
        edge_out[1, c : c + 1] = own[c][CELLS - 1 : CELLS]
    halo = [
        remote(x_ref.at[0], x_ref.at[k + 1], halo_s.at[k], halo_r.at[k], (to, p)) for k, to in enumerate((up, down))
    ]
    edges = []
    for side, to_dom, source in ((0, right, 1), (1, left, 0)):
        for k, to_slab in enumerate((s, up, down)):
            e = side * 3 + k
            edges.append(remote(edge_out.at[source], edge_in.at[e], edge_s.at[e], edge_r.at[e], (to_slab, to_dom)))
    early = [remote(x_ref.at[0], bx_ref, early_s.at[0], early_r.at[0], (other, p))]
    for copy in halo + edges + early:
        copy.start()

    def prepare(k):
        xs = [x_ref[k, c] * KAP for c in range(3)]
        m = x_ref[k, 3]
        n = xs[0] * xs[0] + xs[1] * xs[1] + xs[2] * xs[2]
        if k == 0:
            inner = pl.ds(8, CELLS)
            for c in range(3):
                xi_ref[c, inner] = xs[c]
            xi_ref[3, inner] = n + C0
            xi_ref[4, inner] = m
        for c, row in enumerate([xs[0] * -2.0, xs[1] * -2.0, xs[2] * -2.0, n]):
            j_ref[pl.ds(c, CELLS, stride=8), :] = row
            j_ref[pl.ds(c + 4, CELLS, stride=8), :] = row
        for c, row in enumerate([xs[0] * m, xs[1] * m, xs[2] * m, m]):
            head = rounded(row)
            w_ref[k, pl.ds(c, CELLS, stride=8), :] = head
            w_ref[k, pl.ds(c + 4, CELLS, stride=8), :] = row - head
        for g in range(CELLS // 16):
            tt_ref[k, g] = j_ref[pl.ds(g * 128, 128), :].T

    zero8 = jnp.zeros((8, TILE), F32)

    def spread(table, base, slot):
        for c in range(4):
            lb_ref[slot, c] = jnp.take_along_axis(table, jnp.full((TILE, TILE), base + c, jnp.int32), axis=1)

    def stage(k, n, slot):
        spread(tt_ref[k, n // 16], lax.rem(n, 16) * 8, slot)

    def pairs(weights, slot, centres):
        weights = jnp.concatenate([weights, zero8], axis=0).astype(BF16)
        ax, ay, az, nj = [lb_ref[slot, c] for c in range(4)]
        for i in centres:
            x, y, z, n = [xi_ref[c, pl.ds(i + 8, 1), :] for c in range(4)]
            u = ((ax * x + ay * y) + (az * z + nj)) + n
            w = jnp.exp2(jnp.log2(u) * -1.5 - u)
            head = w.astype(BF16)
            rest = (w - head.astype(F32)).astype(BF16)
            pull = jnp.dot(weights, head, preferred_element_type=F32) + jnp.dot(weights, rest, preferred_element_type=F32)
            acc_ref[pl.ds(pl.multiple_of((i + 9) * 8, 8), 8), :] += pull[:8]

    def cell(k, n, slot):
        pairs(w_ref[k, pl.ds(pl.multiple_of(n * 8, 8), 8), :], slot, (n - 1, n, n + 1))

    prepare(0)
    stage(0, 0, 0)

    def inner_slab(step, carry):
        for i in range(UNROLL):
            n = step * UNROLL + i
            stage(0, jnp.minimum(n + 1, CELLS - 1), (i + 1) % UNROLL)
            cell(0, n, i)
        return carry

    lax.fori_loop(0, CELLS // UNROLL, inner_slab, 0)

    speed = merged(1, 3)
    for c in range(3):
        v_ref[c] = speed[c]
    early.append(remote(v_ref, bv_ref, early_s.at[1], early_r.at[1], (other, p)))
    early[1].start()

    for e, copy in enumerate(edges):
        copy.wait_recv()
        tile = edge_in[e]
        xs = [tile[c : c + 1] * KAP for c in range(3)]
        m = tile[3:4]
        n = xs[0] * xs[0] + xs[1] * xs[1] + xs[2] * xs[2]
        for c, row in enumerate([xs[0] * -2.0, xs[1] * -2.0, xs[2] * -2.0, n]):
            je_ref[e * 8 + c : e * 8 + c + 1] = row
        for c, row in enumerate([xs[0] * m, xs[1] * m, xs[2] * m, m]):
            head = rounded(row)
            we_ref[e * 8 + c : e * 8 + c + 1] = head
            we_ref[e * 8 + c + 4 : e * 8 + c + 5] = row - head
    te_ref[...] = je_ref[...].T
    for e in range(6):
        spread(te_ref[...], e * 8, e)
        pairs(we_ref[e * 8 : e * 8 + 8], e, (0 if e < 3 else CELLS - 1,))

    for k, copy in enumerate(halo):
        copy.wait_recv()
        prepare(k + 1)

    def finish(row):
        total = []
        for c in range(4):
            at = pl.multiple_of((row + 1) * 8, 8)
            total.append(acc_ref[pl.ds(at + c, 8, stride=8), :] + acc_ref[pl.ds(at + c + 4, 8, stride=8), :])
        live = xi_ref[4, pl.ds(row, 8)] > 0
        for c in range(3):
            pull = (total[c] - xi_ref[c, pl.ds(row, 8)] * total[3]) * SCALE
            ac_ref[c, pl.ds(row, 8)] = jnp.where(live, pull, 0.0)

    def late(k, rows):
        part = pl.ds(pl.multiple_of(k * 16, 8), rows)
        return remote(ac_ref.at[:, part], ba_ref.at[:, part], late_s.at[k], late_r.at[k], (other, p))

    per_step = UNROLL // 2
    stage(1, 0, 0)

    def chunk(k, carry):
        def outer_slabs(step, carry):
            for i in range(per_step):
                n = k * 16 + step * per_step + i
                stage(2, n, (2 * i + 1) % UNROLL)
                cell(1, n, 2 * i)
                stage(1, jnp.minimum(n + 1, CELLS - 1), (2 * i + 2) % UNROLL)
                cell(2, n, 2 * i + 1)
            return carry

        lax.fori_loop(0, 16 // per_step, outer_slabs, 0)
        row = pl.multiple_of(k * 16, 8)
        finish(row)
        finish(row + 8)
        late(k, 16).start()
        return carry

    lax.fori_loop(0, CELLS // 16, chunk, 0)
    finish(CELLS)
    last = CELLS // 16
    late(last, 8).start()

    state_ref[0:4] = x_ref[0]
    accel = ac_ref[:, 8:]
    state_ref[4:7] = v_ref[...] + kick_step * accel
    state_ref[7:10] = accel
    for copy in early:
        copy.wait_recv()
    for k in range(last + 1):
        late(k, 16 if k < last else 8).wait_recv()
    buddy_ref[0:4] = bx_ref[...]
    accel = ba_ref[:, 8:]
    buddy_ref[4:7] = bv_ref[...] + kick_step * accel
    buddy_ref[7:10] = accel
    for copy in route[0] + route[1] + halo + edges + early:
        copy.wait_send()
    for k in range(last + 1):
        late(k, 16 if k < last else 8).wait_send()


def per_device(positions, velocities, masses, owner_cell, counts):
    n_slab, n_dom = lax.axis_size("slab"), lax.axis_size("dom")
    vmem = pl.BlockSpec(memory_space=pltpu.VMEM)
    out = jax.ShapeDtypeStruct((10, CELLS, TILE), F32)
    block = (CELLS, TILE)
    dma = pltpu.SemaphoreType.DMA
    state, buddy = pl.pallas_call(
        functools.partial(kernel, n_slab, n_dom),
        out_shape=(out, out),
        in_specs=[vmem] * 4 + [pl.BlockSpec(memory_space=pltpu.SMEM)],
        out_specs=(vmem, vmem),
        scratch_shapes=[
            pltpu.VMEM((PARTS * 224, GROUP * BLOCK), BF16),
            pltpu.VMEM((256, GROUP * BLOCK), BF16),
            pltpu.VMEM((PARTS * 224, 256), F32),
            pltpu.VMEM((2, 256, 128), F32),
            pltpu.VMEM((2, 3, *block), F32),
            pltpu.VMEM((3, 4, *block), F32),
            pltpu.VMEM((2, 8, TILE), F32),
            pltpu.VMEM((6, 8, TILE), F32),
            pltpu.VMEM((3, *block), F32),
            pltpu.VMEM((3, CELLS + 8, TILE), F32),
            pltpu.VMEM((4, *block), F32),
            pltpu.VMEM((3, *block), F32),
            pltpu.VMEM((3, CELLS + 8, TILE), F32),
            pltpu.VMEM((5, CELLS + 16, TILE), F32),
            pltpu.VMEM((CELLS * 8, TILE), F32),
            pltpu.VMEM((3, CELLS * 8, TILE), F32),
            pltpu.VMEM((3, CELLS // 16, TILE, TILE), F32),
            pltpu.VMEM((TILE, TILE), F32),
            pltpu.VMEM((48, TILE), F32),
            pltpu.VMEM((TILE, TILE), F32),
            pltpu.VMEM(((CELLS + 10) * 8, TILE), F32),
            pltpu.VMEM((UNROLL, 4, TILE, TILE), F32),
            dma((2, 3)), dma((2, 3)), dma((2,)), dma((2,)), dma((6,)), dma((6,)), dma((2,)), dma((2,)), dma((5,)), dma((5,)),
        ],
        compiler_params=pltpu.CompilerParams(collective_id=0, has_side_effects=True),
        name="substep",
    )(positions, velocities, masses.reshape(1, -1), owner_cell.reshape(1, -1), counts)
    return state[:, None], buddy[:, None]


def solution(mesh):
    placed = (
        P(None, ("slab", "dom")),
        P(None, ("slab", "dom")),
        P(("slab", "dom")),
        P(("slab", "dom"), None),
        P(("slab", "dom")),
    )
    return jax.shard_map(
        per_device,
        mesh=mesh,
        in_specs=placed,
        out_specs=(P(None, "slab", "dom", None), P(None, "slab", "dom", None)),
        check_vma=False,
    )
```

time: 176 us -> 75.3 us (0.43)
  the two profiles are of different devices: /device:TPU:63 before, /device:TPU:128 now
where the time goes in v1:
time: 75.3 us; the launch traced here: 75.1 us
  Pallas kernels  71.3 us (95%)
  local copies, waits for them, and re-layouts  2.5 us (3%)
  between operations  1.29 us (2%)
    pallas_call x1, Pallas kernels, per_device(): pl.pallas_call(functools.partial(kernel, n_slab, n_dom), out_shape=(out,...  71.3 us
    unnamed x4, local copies, waits for them, and re-layouts  2.5 us

profile of v1, /device:TPU:128, one launch (start us, length us, event | category | flops | bytes accessed | tf_op | source)
XLA Modules:
  0.0 75.1 jit_solution(308652191471649069)
XLA Ops:
  1.3 71.3 %substep.1 = (f32[10,64,128]{2,1,0:T(8,128)}, f32[10,64,128]{2,1,0:T(8,128)}) custom-call(f32[3,6144]{1,0:T(4,128)} %pos_ref.1, f32[3,6144]{1,0:T(4,128)} %vel_ref.1, f32[1,6144]{1,0:T(1,128)} %bitcast.10, s32[1,6144]{1,0:T(1,128)} %bitcast.11, s32[1]{0:T(128)S(6)} %copy.11.cnt_ref), custom_call_target="tpu_custom_call" | custom-call | tf_op jit(solution)/shard_map/substep/pallas_call | solution.py:301
  72.6 0.0 copy-start
  72.6 1.8 %copy.12 = f32[10,1,64,128]{3,2,1,0:T(8,128)} copy(f32[10,1,64,128]{3,2,1,0:T(8,128)} %bitcast.9) | data formatting | bytes 655360
  74.4 0.0 copy-done
  74.4 0.7 copy.13
Async XLA Ops:
  72.6 1.8 %copy-start = (f32[10,64,128]{2,1,0:T(8,128)S(1)}, f32[10,64,128]{2,1,0:T(8,128)}, u32[]{:S(2)}) copy-start(f32[10,64,128]{2,1,0:T(8,128)} %get-tuple-element.5) | copy-start | bytes 983044

commit v2 on v1

--- a/solution.py
+++ b/solution.py
@@ -12,9 +12,12 @@
 TILE = 128
 SLOT = 32
 BLOCK = 256
-GROUP = 4
-PARTS = 3
-UNROLL = 8
+GROUP = 8
+PARTS = 2
+UNROLL = 16
+VMEM_LIMIT = 24 << 20
+DELAY = 2
+FAR = 8
 F32, BF16 = jnp.float32, jnp.bfloat16
 MESH = pl.DeviceIdType.MESH
 
@@ -32,7 +35,7 @@
     return x.astype(BF16).astype(F32)
 
 
-def place_rows(pos_ref, vel_ref, mass_ref, own_ref, cnt_ref, a_ref, b_ref, d_ref):
+def place_rows(pos_ref, vel_ref, mass_ref, own_ref, cnt_ref, a_ref, av_ref, b_ref, d_ref):
     rows = pos_ref.shape[1]
     before = lax.broadcasted_iota(jnp.int32, (BLOCK, BLOCK), 0) < lax.broadcasted_iota(jnp.int32, (BLOCK, BLOCK), 1)
     tri = jnp.concatenate([before.astype(BF16), jnp.ones((BLOCK, 128), BF16)], axis=1)
@@ -43,36 +46,53 @@
     d_ref[...] = jnp.zeros_like(d_ref)
 
     def group(g, prefix):
+        whole = pl.ds(pl.multiple_of(g * GROUP * BLOCK, BLOCK), GROUP * BLOCK)
         for q in range(GROUP):
             off = pl.multiple_of((g * GROUP + q) * BLOCK, BLOCK)
-            here = pl.ds(q * BLOCK, BLOCK)
-            hot = owner == jnp.where(lane + off < live, own_ref[:, pl.ds(off, BLOCK)], -1)
+            rows_here = pl.ds(off, BLOCK)
+            hot = owner == jnp.where(lane + off < live, own_ref[:, rows_here], -1)
             hot16 = jnp.where(hot, 1.0, 0.0).astype(BF16)
-            b_ref[:, here] = hot16
+            b_ref[:, rows_here] = hot16
             seen = jnp.dot(hot16, tri, preferred_element_type=F32)
             earlier = seen[:, :BLOCK] + jnp.concatenate([prefix, prefix], axis=1)
             prefix = prefix + seen[:, BLOCK:]
             rank = ranks == jnp.sum(jnp.where(hot, earlier, 0.0), axis=0, keepdims=True)
-            v = vel_ref[:, pl.ds(off, BLOCK)]
-            x = pos_ref[:, pl.ds(off, BLOCK)] + drift_step * v
-            values = [x[0:1], x[1:2], x[2:3], mass_ref[:, pl.ds(off, BLOCK)], v[0:1], v[1:2], v[2:3]]
-            for c, value in enumerate(values):
-                for piece in range(PARTS):
-                    head = rounded(value)
-                    a_ref[pl.ds((piece * 7 + c) * SLOT, SLOT), here] = jnp.where(rank, head, 0.0).astype(BF16)
-                    value = value - head
-        d_ref[...] += lax.dot_general(a_ref[...], b_ref[...], (((1,), (1,)), ((), ())), preferred_element_type=F32)
+
+            def put(ref, values, where):
+                for c, value in enumerate(values):
+                    for piece in range(PARTS):
+                        head = rounded(value)
+                        at = pl.ds((piece * len(values) + c) * SLOT, SLOT)
+                        ref[at, where] = jnp.where(rank, head, 0.0).astype(BF16)
+                        value = value - head
+
+            v = vel_ref[:, rows_here]
+            x = pos_ref[:, rows_here] + drift_step * v
+            put(a_ref, [x[0:1], x[1:2], x[2:3], mass_ref[:, rows_here]], pl.ds(q * BLOCK, BLOCK))
+            put(av_ref, [v[0:1], v[1:2], v[2:3]], rows_here)
+        d_ref[...] += product(a_ref[...], b_ref[:, whole])
         return prefix
 
     lax.fori_loop(0, rows // (GROUP * BLOCK), group, jnp.zeros((256, 128), F32))
+
+
+def product(a, b):
+    return lax.dot_general(a, b, (((1,), (1,)), ((), ())), preferred_element_type=F32)
+
+
+def summed(pieces, size):
+    total = pieces[0:size]
+    for piece in range(1, PARTS):
+        total = total + pieces[piece * size : (piece + 1) * size]
+    return total
 
 
 def kernel(
     n_slab, n_dom,
     pos_ref, vel_ref, mass_ref, own_ref, cnt_ref, state_ref, buddy_ref,
-    a_ref, b_ref, d_ref, sent_ref, got_ref, x_ref, edge_out, edge_in, v_ref, ac_ref, bx_ref, bv_ref, ba_ref,
-    xi_ref, j_ref, w_ref, tt_ref, je_ref, we_ref, te_ref, acc_ref, lb_ref,
-    route_s, route_r, halo_s, halo_r, edge_s, edge_r, early_s, early_r, late_s, late_r,
+    a_ref, av_ref, b_ref, d_ref, sent_ref, got_ref, x_ref, edge_out, edge_in, v_ref, ac_ref, bx_ref, bv_ref, ba_ref,
+    sv_ref, bw_ref, xi_ref, j_ref, w_ref, tt_ref, je_ref, we_ref, te_ref, acc_ref, lb_ref,
+    route_s, route_r, halo_s, halo_r, edge_s, edge_r, early_s, early_r, late_s, late_r, out_s,
 ):
     s, p = lax.axis_index("slab"), lax.axis_index("dom")
     up, down = lax.rem(s + 1, n_slab), lax.rem(s + n_slab - 1, n_slab)
@@ -86,17 +106,13 @@
     for peer in peers:
         pl.semaphore_signal(barrier, inc=1, device_id=peer, device_id_type=MESH)
 
-    place_rows(pos_ref, vel_ref, mass_ref, own_ref, cnt_ref, a_ref, b_ref, d_ref)
-    placed = d_ref[0:224]
-    for piece in range(1, PARTS):
-        placed = placed + d_ref[piece * 224 : piece * 224 + 224]
-    for half in range(2):
-        cols = slice(half * 128, half * 128 + 128)
-        first = placed[0:128, cols].T
-        second = jnp.concatenate([placed[128:224, cols], jnp.zeros((32, 128), F32)], axis=0).T
-        sent_ref[0, cols] = pltpu.roll(first, p * SLOT, 1)
-        sent_ref[1, cols] = pltpu.roll(second, p * SLOT, 1)
-
+    place_rows(pos_ref, vel_ref, mass_ref, own_ref, cnt_ref, a_ref, av_ref, b_ref, d_ref)
+
+    def pack(half, placed):
+        for cols in (slice(0, 128), slice(128, 256)):
+            sent_ref[half, cols] = pltpu.roll(placed[:, cols].T, p * SLOT, 1)
+
+    pack(0, summed(d_ref[...], 4 * SLOT))
     pl.semaphore_wait(barrier, len(peers))
 
     def remote(src, dst, send, recv, device):
@@ -105,7 +121,8 @@
         )
 
     route = [[], []]
-    for half in range(2):
+
+    def send_rows(half):
         for t in range(1, n_dom):
             q = lax.rem(p + t, n_dom)
             copy = remote(
@@ -115,6 +132,10 @@
             copy.start()
             route[half].append(copy)
 
+    send_rows(0)
+    speeds = summed(product(av_ref[...], b_ref[...]), 3 * SLOT)
+    pack(1, jnp.concatenate([speeds, jnp.zeros((SLOT, 256), F32)], axis=0))
+    send_rows(1)
     acc_ref[...] = jnp.zeros_like(acc_ref)
     xi_ref[...] = jnp.full(xi_ref.shape, C0, F32)
     xi_ref[4] = jnp.zeros(xi_ref.shape[1:], F32)
@@ -148,15 +169,19 @@
         for k, to_slab in enumerate((s, up, down)):
             e = side * 3 + k
             edges.append(remote(edge_out.at[source], edge_in.at[e], edge_s.at[e], edge_r.at[e], (to_slab, to_dom)))
+    for copy in halo + edges:
+        copy.start()
+    outs = [pltpu.make_async_copy(x_ref.at[0], state_ref.at[0:4], out_s.at[0])]
+    outs[0].start()
     early = [remote(x_ref.at[0], bx_ref, early_s.at[0], early_r.at[0], (other, p))]
-    for copy in halo + edges + early:
-        copy.start()
+    crossing = lax.rem(s + 2, 2 * FAR) < 4
+    turn = jnp.where(crossing, DELAY, 0)
 
     def prepare(k):
         xs = [x_ref[k, c] * KAP for c in range(3)]
         m = x_ref[k, 3]
         n = xs[0] * xs[0] + xs[1] * xs[1] + xs[2] * xs[2]
-        if k == 0:
+        if isinstance(k, int):
             inner = pl.ds(8, CELLS)
             for c in range(3):
                 xi_ref[c, inner] = xs[c]
@@ -196,23 +221,41 @@
     def cell(k, n, slot):
         pairs(w_ref[k, pl.ds(pl.multiple_of(n * 8, 8), 8), :], slot, (n - 1, n, n + 1))
 
+    def whole_slab(k, own=False):
+        def step(t, carry):
+            if own:
+
+                @pl.when(t == turn)
+                def _():
+                    early[0].start()
+
+            for i in range(UNROLL):
+                n = t * UNROLL + i
+                stage(k, jnp.minimum(n + 1, CELLS - 1), (i + 1) % UNROLL)
+                cell(k, n, i)
+            return carry
+
+        stage(k, 0, 0)
+        lax.fori_loop(0, CELLS // UNROLL, step, 0)
+
     prepare(0)
-    stage(0, 0, 0)
-
-    def inner_slab(step, carry):
-        for i in range(UNROLL):
-            n = step * UNROLL + i
-            stage(0, jnp.minimum(n + 1, CELLS - 1), (i + 1) % UNROLL)
-            cell(0, n, i)
-        return carry
-
-    lax.fori_loop(0, CELLS // UNROLL, inner_slab, 0)
+    whole_slab(0, own=True)
 
     speed = merged(1, 3)
     for c in range(3):
         v_ref[c] = speed[c]
     early.append(remote(v_ref, bv_ref, early_s.at[1], early_r.at[1], (other, p)))
     early[1].start()
+
+    near = jnp.where(lax.rem(s, FAR) == 0, 2, 1)
+    far = 3 - near
+
+    def arrived(k):
+        remote(x_ref.at[0], x_ref.at[k], halo_s.at[k - 1], halo_r.at[k - 1], (up, p)).wait_recv()
+
+    arrived(near)
+    prepare(near)
+    whole_slab(near)
 
     for e, copy in enumerate(edges):
         copy.wait_recv()
@@ -231,9 +274,8 @@
         spread(te_ref[...], e * 8, e)
         pairs(we_ref[e * 8 : e * 8 + 8], e, (0 if e < 3 else CELLS - 1,))
 
-    for k, copy in enumerate(halo):
-        copy.wait_recv()
-        prepare(k + 1)
+    arrived(far)
+    prepare(far)
 
     def finish(row):
         total = []
@@ -249,20 +291,17 @@
         part = pl.ds(pl.multiple_of(k * 16, 8), rows)
         return remote(ac_ref.at[:, part], ba_ref.at[:, part], late_s.at[k], late_r.at[k], (other, p))
 
-    per_step = UNROLL // 2
-    stage(1, 0, 0)
+    stage(far, 0, 0)
 
     def chunk(k, carry):
-        def outer_slabs(step, carry):
-            for i in range(per_step):
-                n = k * 16 + step * per_step + i
-                stage(2, n, (2 * i + 1) % UNROLL)
-                cell(1, n, 2 * i)
-                stage(1, jnp.minimum(n + 1, CELLS - 1), (2 * i + 2) % UNROLL)
-                cell(2, n, 2 * i + 1)
+        def step(t, carry):
+            for i in range(UNROLL):
+                n = k * 16 + t * UNROLL + i
+                stage(far, jnp.minimum(n + 1, CELLS - 1), (i + 1) % UNROLL)
+                cell(far, n, i)
             return carry
 
-        lax.fori_loop(0, 16 // per_step, outer_slabs, 0)
+        lax.fori_loop(0, 16 // UNROLL, step, 0)
         row = pl.multiple_of(k * 16, 8)
         finish(row)
         finish(row + 8)
@@ -274,18 +313,24 @@
     last = CELLS // 16
     late(last, 8).start()
 
-    state_ref[0:4] = x_ref[0]
-    accel = ac_ref[:, 8:]
-    state_ref[4:7] = v_ref[...] + kick_step * accel
-    state_ref[7:10] = accel
+    def store(src, dst):
+        outs.append(pltpu.make_async_copy(src, dst, out_s.at[len(outs)]))
+        outs[-1].start()
+
+    inner = pl.ds(8, CELLS)
+    sv_ref[...] = v_ref[...] + kick_step * ac_ref[:, inner]
+    store(sv_ref, state_ref.at[4:7])
+    store(ac_ref.at[:, inner], state_ref.at[7:10])
     for copy in early:
         copy.wait_recv()
+    store(bx_ref, buddy_ref.at[0:4])
     for k in range(last + 1):
         late(k, 16 if k < last else 8).wait_recv()
-    buddy_ref[0:4] = bx_ref[...]
-    accel = ba_ref[:, 8:]
-    buddy_ref[4:7] = bv_ref[...] + kick_step * accel
-    buddy_ref[7:10] = accel
+    store(ba_ref.at[:, inner], buddy_ref.at[7:10])
+    bw_ref[...] = bv_ref[...] + kick_step * ba_ref[:, inner]
+    store(bw_ref, buddy_ref.at[4:7])
+    for copy in outs:
+        copy.wait()
     for copy in route[0] + route[1] + halo + edges + early:
         copy.wait_send()
     for k in range(last + 1):
@@ -294,6 +339,7 @@
 
 def per_device(positions, velocities, masses, owner_cell, counts):
     n_slab, n_dom = lax.axis_size("slab"), lax.axis_size("dom")
+    rows = positions.shape[1]
     vmem = pl.BlockSpec(memory_space=pltpu.VMEM)
     out = jax.ShapeDtypeStruct((10, CELLS, TILE), F32)
     block = (CELLS, TILE)
@@ -302,11 +348,12 @@
         functools.partial(kernel, n_slab, n_dom),
         out_shape=(out, out),
         in_specs=[vmem] * 4 + [pl.BlockSpec(memory_space=pltpu.SMEM)],
-        out_specs=(vmem, vmem),
+        out_specs=(pl.BlockSpec(memory_space=pl.ANY),) * 2,
         scratch_shapes=[
-            pltpu.VMEM((PARTS * 224, GROUP * BLOCK), BF16),
-            pltpu.VMEM((256, GROUP * BLOCK), BF16),
-            pltpu.VMEM((PARTS * 224, 256), F32),
+            pltpu.VMEM((PARTS * 4 * SLOT, GROUP * BLOCK), BF16),
+            pltpu.VMEM((PARTS * 3 * SLOT, rows), BF16),
+            pltpu.VMEM((256, rows), BF16),
+            pltpu.VMEM((PARTS * 4 * SLOT, 256), F32),
             pltpu.VMEM((2, 256, 128), F32),
             pltpu.VMEM((2, 3, *block), F32),
             pltpu.VMEM((3, 4, *block), F32),
@@ -317,6 +364,8 @@
             pltpu.VMEM((4, *block), F32),
             pltpu.VMEM((3, *block), F32),
             pltpu.VMEM((3, CELLS + 8, TILE), F32),
+            pltpu.VMEM((3, *block), F32),
+            pltpu.VMEM((3, *block), F32),
             pltpu.VMEM((5, CELLS + 16, TILE), F32),
             pltpu.VMEM((CELLS * 8, TILE), F32),
             pltpu.VMEM((3, CELLS * 8, TILE), F32),
@@ -326,9 +375,9 @@
             pltpu.VMEM((TILE, TILE), F32),
             pltpu.VMEM(((CELLS + 10) * 8, TILE), F32),
             pltpu.VMEM((UNROLL, 4, TILE, TILE), F32),
-            dma((2, 3)), dma((2, 3)), dma((2,)), dma((2,)), dma((6,)), dma((6,)), dma((2,)), dma((2,)), dma((5,)), dma((5,)),
+            dma((2, 3)), dma((2, 3)), dma((2,)), dma((2,)), dma((6,)), dma((6,)), dma((2,)), dma((2,)), dma((5,)), dma((5,)), dma((6,)),
         ],
-        compiler_params=pltpu.CompilerParams(collective_id=0, has_side_effects=True),
+        compiler_params=pltpu.CompilerParams(collective_id=0, has_side_effects=True, vmem_limit_bytes=VMEM_LIMIT),
         name="substep",
     )(positions, velocities, masses.reshape(1, -1), owner_cell.reshape(1, -1), counts)
     return state[:, None], buddy[:, None]

time: 75.3 us -> 58.6 us (0.78)
  the two profiles are of different devices: /device:TPU:128 before, /device:TPU:110 now
where the time goes in v2:
time: 58.6 us; the launch traced here: 58.3 us
  Pallas kernels  52.3 us (89%)
  local copies, waits for them, and re-layouts  4.7 us (8%)
  between operations  1.3 us (2%)
    pallas_call x1, Pallas kernels, per_device(): pl.pallas_call(functools.partial(kernel, n_slab, n_dom), out_shape=(out,...  52.3 us
    unnamed x10, local copies, waits for them, and re-layouts  4.7 us

profile of v2, /device:TPU:110, one launch (start us, length us, event | category | flops | bytes accessed | tf_op | source)
XLA Modules:
  0.0 58.3 jit_solution(1341267174287319833)
XLA Ops:
  1.3 0.0 copy-start
  1.3 0.9 %copy-done = f32[3,6144]{1,0:T(4,128)S(1)} copy-done((f32[3,6144]{1,0:T(4,128)S(1)}, f32[3,6144]{1,0:T(4,128)}, u32[]{:S(2)}) %copy-start) | copy-done | bytes 73752
  2.2 0.0 copy-start.1
  2.2 0.9 %copy-done.1 = f32[3,6144]{1,0:T(4,128)S(1)} copy-done((f32[3,6144]{1,0:T(4,128)S(1)}, f32[3,6144]{1,0:T(4,128)}, u32[]{:S(2)}) %copy-start.1) | copy-done | bytes 73752
  3.1 0.0 copy-start.2
  3.1 0.7 %copy-done.2 = f32[6144]{0:T(1024)S(1)} copy-done((f32[6144]{0:T(1024)S(1)}, f32[6144]{0:T(1024)}, u32[]{:S(2)}) %copy-start.2) | copy-done | bytes 24600
  3.8 0.0 copy-start.3
  3.8 0.7 %copy-done.3 = s32[6144,1]{0,1:T(1,128)S(1)} copy-done((s32[6144,1]{0,1:T(1,128)S(1)}, s32[6144,1]{0,1:T(1,128)}, u32[]{:S(2)}) %copy-start.3) | copy-done | bytes 24600
  4.5 52.3 %substep.1 = (f32[10,64,128]{2,1,0:T(8,128)S(1)}, f32[10,64,128]{2,1,0:T(8,128)S(1)}) custom-call(f32[3,6144]{1,0:T(4,128)S(1)} %copy-done, f32[3,6144]{1,0:T(4,128)S(1)} %copy-done.1, f32[1,6144]{1,0:T(1,128)S(1)} %bitcast.10, s32[1,6144]{1,0:T(1,128)S(1)} %bitcast.11, s32[1]{0:T(128)S(6)} %copy.11.cnt_ref), custom_call_target="tpu_custom_call" | custom-call | tf_op jit(solution)/shard_map/substep/pallas_call | solution.py:347
  56.9 0.7 %copy.12 = f32[10,1,64,128]{3,2,1,0:T(8,128)} copy(f32[10,1,64,128]{3,2,1,0:T(8,128)S(1)} %bitcast.9) | data formatting | bytes 655360
  57.6 0.7 %copy.13 = f32[10,1,64,128]{3,2,1,0:T(8,128)} copy(f32[10,1,64,128]{3,2,1,0:T(8,128)S(1)} %bitcast.8) | data formatting | bytes 655360
Async XLA Ops:
  1.3 0.9 %copy-start = (f32[3,6144]{1,0:T(4,128)S(1)}, f32[3,6144]{1,0:T(4,128)}, u32[]{:S(2)}) copy-start(f32[3,6144]{1,0:T(4,128)} %pos_ref.1) | copy-start | bytes 221188
  2.2 0.9 %copy-start.1 = (f32[3,6144]{1,0:T(4,128)S(1)}, f32[3,6144]{1,0:T(4,128)}, u32[]{:S(2)}) copy-start(f32[3,6144]{1,0:T(4,128)} %vel_ref.1) | copy-start | bytes 221188
  3.1 0.7 %copy-start.2 = (f32[6144]{0:T(1024)S(1)}, f32[6144]{0:T(1024)}, u32[]{:S(2)}) copy-start(f32[6144]{0:T(1024)} %param.7) | copy-start | bytes 73732
  3.8 0.7 %copy-start.3 = (s32[6144,1]{0,1:T(1,128)S(1)}, s32[6144,1]{0,1:T(1,128)}, u32[]{:S(2)}) copy-start(s32[6144,1]{0,1:T(1,128)} %param.8) | copy-start | bytes 73732

commit v3 on v2

--- a/solution.py
+++ b/solution.py
@@ -89,16 +89,20 @@
 
 def kernel(
     n_slab, n_dom,
-    pos_ref, vel_ref, mass_ref, own_ref, cnt_ref, state_ref, buddy_ref,
+    pos_hbm, vel_hbm, mass_hbm, own_hbm, cnt_ref, state_ref, buddy_ref, pos_ref, vel_ref, mass_ref, own_ref,
     a_ref, av_ref, b_ref, d_ref, sent_ref, got_ref, x_ref, edge_out, edge_in, v_ref, ac_ref, bx_ref, bv_ref, ba_ref,
     sv_ref, bw_ref, xi_ref, j_ref, w_ref, tt_ref, je_ref, we_ref, te_ref, acc_ref, lb_ref,
-    route_s, route_r, halo_s, halo_r, edge_s, edge_r, early_s, early_r, late_s, late_r, out_s,
+    route_s, route_r, halo_s, halo_r, edge_s, edge_r, early_s, early_r, late_s, late_r, out_s, in_s,
 ):
     s, p = lax.axis_index("slab"), lax.axis_index("dom")
     up, down = lax.rem(s + 1, n_slab), lax.rem(s + n_slab - 1, n_slab)
     right, left = lax.rem(p + 1, n_dom), lax.rem(p + n_dom - 1, n_dom)
     other = lax.rem(s + n_slab // 2, n_slab)
 
+    pairs_in = ((own_hbm, own_ref), (pos_hbm, pos_ref), (vel_hbm, vel_ref), (mass_hbm, mass_ref))
+    loads = [pltpu.make_async_copy(src, dst, in_s.at[i]) for i, (src, dst) in enumerate(pairs_in)]
+    for copy in loads:
+        copy.start()
     barrier = pltpu.get_barrier_semaphore()
     peers = [(s, lax.rem(p + t, n_dom)) for t in range(1, n_dom)]
     peers += [(a, b) for a in (up, down) for b in (p, left, right)]
@@ -106,6 +110,13 @@
     for peer in peers:
         pl.semaphore_signal(barrier, inc=1, device_id=peer, device_id_type=MESH)
 
+    acc_ref[...] = jnp.zeros_like(acc_ref)
+    xi_ref[...] = jnp.full(xi_ref.shape, C0, F32)
+    xi_ref[4] = jnp.zeros(xi_ref.shape[1:], F32)
+    edge_out[...] = jnp.zeros_like(edge_out)
+    je_ref[...] = jnp.zeros_like(je_ref)
+    for copy in loads:
+        copy.wait()
     place_rows(pos_ref, vel_ref, mass_ref, own_ref, cnt_ref, a_ref, av_ref, b_ref, d_ref)
 
     def pack(half, placed):
@@ -136,11 +147,6 @@
     speeds = summed(product(av_ref[...], b_ref[...]), 3 * SLOT)
     pack(1, jnp.concatenate([speeds, jnp.zeros((SLOT, 256), F32)], axis=0))
     send_rows(1)
-    acc_ref[...] = jnp.zeros_like(acc_ref)
-    xi_ref[...] = jnp.full(xi_ref.shape, C0, F32)
-    xi_ref[4] = jnp.zeros(xi_ref.shape[1:], F32)
-    edge_out[...] = jnp.zeros_like(edge_out)
-    je_ref[...] = jnp.zeros_like(je_ref)
     lane_group = lax.broadcasted_iota(jnp.int32, (CELLS, TILE), 1) // SLOT
 
     def merged(half, count):
@@ -337,19 +343,33 @@
         late(k, 16 if k < last else 8).wait_send()
 
 
+def written(state_ref, buddy_ref, state_out, buddy_out, sem):
+    copies = [
+        pltpu.make_async_copy(state_ref, state_out, sem.at[0]),
+        pltpu.make_async_copy(buddy_ref, buddy_out, sem.at[1]),
+    ]
+    for copy in copies:
+        copy.start()
+    for copy in copies:
+        copy.wait()
+
+
 def per_device(positions, velocities, masses, owner_cell, counts):
     n_slab, n_dom = lax.axis_size("slab"), lax.axis_size("dom")
     rows = positions.shape[1]
-    vmem = pl.BlockSpec(memory_space=pltpu.VMEM)
     out = jax.ShapeDtypeStruct((10, CELLS, TILE), F32)
     block = (CELLS, TILE)
     dma = pltpu.SemaphoreType.DMA
     state, buddy = pl.pallas_call(
         functools.partial(kernel, n_slab, n_dom),
         out_shape=(out, out),
-        in_specs=[vmem] * 4 + [pl.BlockSpec(memory_space=pltpu.SMEM)],
+        in_specs=[pl.BlockSpec(memory_space=pltpu.HBM)] * 4 + [pl.BlockSpec(memory_space=pltpu.SMEM)],
         out_specs=(pl.BlockSpec(memory_space=pl.ANY),) * 2,
         scratch_shapes=[
+            pltpu.VMEM((3, rows), F32),
+            pltpu.VMEM((3, rows), F32),
+            pltpu.VMEM((1, rows), F32),
+            pltpu.VMEM((1, rows), jnp.int32),
             pltpu.VMEM((PARTS * 4 * SLOT, GROUP * BLOCK), BF16),
             pltpu.VMEM((PARTS * 3 * SLOT, rows), BF16),
             pltpu.VMEM((256, rows), BF16),
@@ -375,11 +395,21 @@
             pltpu.VMEM((TILE, TILE), F32),
             pltpu.VMEM(((CELLS + 10) * 8, TILE), F32),
             pltpu.VMEM((UNROLL, 4, TILE, TILE), F32),
-            dma((2, 3)), dma((2, 3)), dma((2,)), dma((2,)), dma((6,)), dma((6,)), dma((2,)), dma((2,)), dma((5,)), dma((5,)), dma((6,)),
+            dma((2, 3)), dma((2, 3)), dma((2,)), dma((2,)), dma((6,)), dma((6,)), dma((2,)), dma((2,)), dma((5,)), dma((5,)), dma((6,)), dma((4,)),
         ],
         compiler_params=pltpu.CompilerParams(collective_id=0, has_side_effects=True, vmem_limit_bytes=VMEM_LIMIT),
         name="substep",
-    )(positions, velocities, masses.reshape(1, -1), owner_cell.reshape(1, -1), counts)
+    )(*[pltpu.with_memory_space_constraint(a, pltpu.HBM) for a in (positions, velocities, masses.reshape(1, -1), owner_cell.reshape(1, -1))], counts)
+    here = pl.BlockSpec(memory_space=pl.ANY)
+    state, buddy = pl.pallas_call(
+        written,
+        out_shape=(out, out),
+        in_specs=[here] * 2,
+        out_specs=(pl.BlockSpec(memory_space=pltpu.HBM),) * 2,
+        scratch_shapes=[dma((2,))],
+        compiler_params=pltpu.CompilerParams(vmem_limit_bytes=1 << 20),
+        name="written",
+    )(state, buddy)
     return state[:, None], buddy[:, None]
 
 

time: 58.6 us -> 59.6 us (1.017)
  the two profiles are of different devices: /device:TPU:110 before, /device:TPU:103 now
where the time goes in v3:
time: 59.6 us; the launch traced here: 59.4 us
  Pallas kernels  58.2 us (98%)
  between operations  1.29 us (2%)
    pallas_call x1, Pallas kernels, per_device(): pl.pallas_call(functools.partial(kernel, n_slab, n_dom), out_shape=(out,...  57.3 us

profile of v3, /device:TPU:103, one launch (start us, length us, event | category | flops | bytes accessed | tf_op | source)
XLA Modules:
  0.0 59.4 jit_solution(15050898231334344057)
XLA Ops:
  1.3 57.3 %substep.1 = (f32[10,64,128]{2,1,0:T(8,128)S(1)}, f32[10,64,128]{2,1,0:T(8,128)S(1)}) custom-call(f32[3,6144]{1,0:T(4,128)} %pos_hbm.1, f32[3,6144]{1,0:T(4,128)} %vel_hbm.1, f32[1,6144]{1,0:T(1,128)} %bitcast.8, s32[1,6144]{1,0:T(1,128)} %bitcast.9, s32[1]{0:T(128)S(6)} %copy.9.cnt_ref), custom_call_target="tpu_custom_call" | custom-call | tf_op jit(solution)/shard_map/substep/pallas_call | solution.py:363
  58.6 0.9 %written.1 = (f32[10,64,128]{2,1,0:T(8,128)}, f32[10,64,128]{2,1,0:T(8,128)}) custom-call(f32[10,64,128]{2,1,0:T(8,128)S(1)} %get-tuple-element.6.state_ref, f32[10,64,128]{2,1,0:T(8,128)S(1)} %get-tuple-element.7.buddy_ref), custom_call_target="tpu_custom_call" | custom-call | tf_op jit(solution)/shard_map/written/pallas_call | solution.py:404

commit v4 on v3

--- a/solution.py
+++ b/solution.py
@@ -16,7 +16,7 @@
 PARTS = 2
 UNROLL = 16
 VMEM_LIMIT = 24 << 20
-DELAY = 2
+SHARED = 32
 FAR = 8
 F32, BF16 = jnp.float32, jnp.bfloat16
 MESH = pl.DeviceIdType.MESH
@@ -91,13 +91,14 @@
     n_slab, n_dom,
     pos_hbm, vel_hbm, mass_hbm, own_hbm, cnt_ref, state_ref, buddy_ref, pos_ref, vel_ref, mass_ref, own_ref,
     a_ref, av_ref, b_ref, d_ref, sent_ref, got_ref, x_ref, edge_out, edge_in, v_ref, ac_ref, bx_ref, bv_ref, ba_ref,
-    sv_ref, bw_ref, xi_ref, j_ref, w_ref, tt_ref, je_ref, we_ref, te_ref, acc_ref, lb_ref,
-    route_s, route_r, halo_s, halo_r, edge_s, edge_r, early_s, early_r, late_s, late_r, out_s, in_s,
+    sv_ref, bw_ref, sa_ref, sb_ref, ae_ref, re_ref, xi_ref, j_ref, w_ref, tt_ref, je_ref, we_ref, te_ref, acc_ref, lb_ref,
+    route_s, route_r, halo_s, halo_r, edge_s, edge_r, early_s, early_r, late_s, late_r, back_s, back_r, out_s, in_s,
 ):
     s, p = lax.axis_index("slab"), lax.axis_index("dom")
     up, down = lax.rem(s + 1, n_slab), lax.rem(s + n_slab - 1, n_slab)
     right, left = lax.rem(p + 1, n_dom), lax.rem(p + n_dom - 1, n_dom)
     other = lax.rem(s + n_slab // 2, n_slab)
+    ahead = s < n_slab // 2
 
     pairs_in = ((own_hbm, own_ref), (pos_hbm, pos_ref), (vel_hbm, vel_ref), (mass_hbm, mass_ref))
     loads = [pltpu.make_async_copy(src, dst, in_s.at[i]) for i, (src, dst) in enumerate(pairs_in)]
@@ -181,11 +182,12 @@
     outs[0].start()
     early = [remote(x_ref.at[0], bx_ref, early_s.at[0], early_r.at[0], (other, p))]
     crossing = lax.rem(s + 2, 2 * FAR) < 4
-    turn = jnp.where(crossing, DELAY, 0)
-
-    def prepare(k):
-        xs = [x_ref[k, c] * KAP for c in range(3)]
-        m = x_ref[k, 3]
+    turn = jnp.where(crossing, jnp.where(ahead, 2, 1), 0)
+
+    def prepare(k, buddy=False):
+        values = [bx_ref[c] if buddy else x_ref[k, c] for c in range(4)]
+        xs = [value * KAP for value in values[:3]]
+        m = values[3]
         n = xs[0] * xs[0] + xs[1] * xs[1] + xs[2] * xs[2]
         if isinstance(k, int):
             inner = pl.ds(8, CELLS)
@@ -242,7 +244,8 @@
             return carry
 
         stage(k, 0, 0)
-        lax.fori_loop(0, CELLS // UNROLL, step, 0)
+        cells = jnp.where(ahead, CELLS, CELLS - SHARED) if own else CELLS
+        lax.fori_loop(0, cells // UNROLL, step, 0)
 
     prepare(0)
     whole_slab(0, own=True)
@@ -283,7 +286,7 @@
     arrived(far)
     prepare(far)
 
-    def finish(row):
+    def finish(row, to):
         total = []
         for c in range(4):
             at = pl.multiple_of((row + 1) * 8, 8)
@@ -291,7 +294,7 @@
         live = xi_ref[4, pl.ds(row, 8)] > 0
         for c in range(3):
             pull = (total[c] - xi_ref[c, pl.ds(row, 8)] * total[3]) * SCALE
-            ac_ref[c, pl.ds(row, 8)] = jnp.where(live, pull, 0.0)
+            to[c, pl.ds(row, 8)] = jnp.where(live, pull, 0.0)
 
     def late(k, rows):
         part = pl.ds(pl.multiple_of(k * 16, 8), rows)
@@ -309,13 +312,13 @@
 
         lax.fori_loop(0, 16 // UNROLL, step, 0)
         row = pl.multiple_of(k * 16, 8)
-        finish(row)
-        finish(row + 8)
+        finish(row, ac_ref)
+        finish(row + 8, ac_ref)
         late(k, 16).start()
         return carry
 
     lax.fori_loop(0, CELLS // 16, chunk, 0)
-    finish(CELLS)
+    finish(CELLS, ac_ref)
     last = CELLS // 16
     late(last, 8).start()
 
@@ -323,17 +326,56 @@
         outs.append(pltpu.make_async_copy(src, dst, out_s.at[len(outs)]))
         outs[-1].start()
 
+    early[0].wait_recv()
+    store(bx_ref, buddy_ref.at[0:4])
+
+    def back(k):
+        part = (pl.ds(SHARED, 16), pl.ds(SHARED + 16, 24))[k]
+        return remote(ae_ref.at[:, part], re_ref.at[:, part], back_s.at[k], back_r.at[k], (other, p))
+
+    @pl.when(ahead)
+    def _():
+        prepare(0, buddy=True)
+        acc_ref[...] = jnp.zeros_like(acc_ref)
+        stage(0, CELLS - SHARED, 0)
+        for k in range(2):
+
+            def step(t, carry, k=k):
+                for i in range(UNROLL):
+                    n = CELLS - SHARED + (k + t) * UNROLL + i
+                    stage(0, jnp.minimum(n + 1, CELLS - 1), (i + 1) % UNROLL)
+                    cell(0, n, i)
+                return carry
+
+            lax.fori_loop(0, 1, step, 0)
+            for row in ((32, 40), (48, 56, 64))[k]:
+                finish(row, ae_ref)
+            back(k).start()
+
     inner = pl.ds(8, CELLS)
-    sv_ref[...] = v_ref[...] + kick_step * ac_ref[:, inner]
+    shared = pl.ds(SHARED, 40)
+    sa_ref[...] = ac_ref[:, inner]
+
+    @pl.when(jnp.logical_not(ahead))
+    def _():
+        for k in range(2):
+            back(k).wait_recv()
+        sa_ref[:, 24:] += re_ref[:, shared]
+
+    sv_ref[...] = v_ref[...] + kick_step * sa_ref[...]
     store(sv_ref, state_ref.at[4:7])
-    store(ac_ref.at[:, inner], state_ref.at[7:10])
-    for copy in early:
-        copy.wait_recv()
-    store(bx_ref, buddy_ref.at[0:4])
+    store(sa_ref, state_ref.at[7:10])
+    early[1].wait_recv()
     for k in range(last + 1):
         late(k, 16 if k < last else 8).wait_recv()
-    store(ba_ref.at[:, inner], buddy_ref.at[7:10])
-    bw_ref[...] = bv_ref[...] + kick_step * ba_ref[:, inner]
+    sb_ref[...] = ba_ref[:, inner]
+
+    @pl.when(ahead)
+    def _():
+        sb_ref[:, 24:] += ae_ref[:, shared]
+
+    store(sb_ref, buddy_ref.at[7:10])
+    bw_ref[...] = bv_ref[...] + kick_step * sb_ref[...]
     store(bw_ref, buddy_ref.at[4:7])
     for copy in outs:
         copy.wait()
@@ -341,6 +383,11 @@
         copy.wait_send()
     for k in range(last + 1):
         late(k, 16 if k < last else 8).wait_send()
+
+    @pl.when(ahead)
+    def _():
+        for k in range(2):
+            back(k).wait_send()
 
 
 def written(state_ref, buddy_ref, state_out, buddy_out, sem):
@@ -386,6 +433,10 @@
             pltpu.VMEM((3, CELLS + 8, TILE), F32),
             pltpu.VMEM((3, *block), F32),
             pltpu.VMEM((3, *block), F32),
+            pltpu.VMEM((3, *block), F32),
+            pltpu.VMEM((3, *block), F32),
+            pltpu.VMEM((3, CELLS + 8, TILE), F32),
+            pltpu.VMEM((3, CELLS + 8, TILE), F32),
             pltpu.VMEM((5, CELLS + 16, TILE), F32),
             pltpu.VMEM((CELLS * 8, TILE), F32),
             pltpu.VMEM((3, CELLS * 8, TILE), F32),
@@ -395,7 +446,7 @@
             pltpu.VMEM((TILE, TILE), F32),
             pltpu.VMEM(((CELLS + 10) * 8, TILE), F32),
             pltpu.VMEM((UNROLL, 4, TILE, TILE), F32),
-            dma((2, 3)), dma((2, 3)), dma((2,)), dma((2,)), dma((6,)), dma((6,)), dma((2,)), dma((2,)), dma((5,)), dma((5,)), dma((6,)), dma((4,)),
+            dma((2, 3)), dma((2, 3)), dma((2,)), dma((2,)), dma((6,)), dma((6,)), dma((2,)), dma((2,)), dma((5,)), dma((5,)), dma((2,)), dma((2,)), dma((6,)), dma((4,)),
         ],
         compiler_params=pltpu.CompilerParams(collective_id=0, has_side_effects=True, vmem_limit_bytes=VMEM_LIMIT),
         name="substep",

time: 59.6 us -> 56.4 us (0.946)
  the two profiles are of different devices: /device:TPU:103 before, /device:TPU:126 now
where the time goes in v4:
time: 56.4 us; the launch traced here: 56.3 us
  Pallas kernels  54.8 us (97%)
  between operations  1.45 us (3%)
    pallas_call x1, Pallas kernels, per_device(): pl.pallas_call(functools.partial(kernel, n_slab, n_dom), out_shape=(out,...  54 us

profile of v4, /device:TPU:126, one launch (start us, length us, event | category | flops | bytes accessed | tf_op | source)
XLA Modules:
  0.0 56.3 jit_solution(3468922921239289733)
XLA Ops:
  1.3 54.0 %substep.1 = (f32[10,64,128]{2,1,0:T(8,128)S(1)}, f32[10,64,128]{2,1,0:T(8,128)S(1)}) custom-call(f32[3,6144]{1,0:T(4,128)} %pos_hbm.1, f32[3,6144]{1,0:T(4,128)} %vel_hbm.1, f32[1,6144]{1,0:T(1,128)} %bitcast.8, s32[1,6144]{1,0:T(1,128)} %bitcast.9, s32[1]{0:T(128)S(6)} %copy.9.cnt_ref), custom_call_target="tpu_custom_call" | custom-call | tf_op jit(solution)/shard_map/substep/pallas_call | solution.py:410
  55.2 0.9 %written.1 = (f32[10,64,128]{2,1,0:T(8,128)}, f32[10,64,128]{2,1,0:T(8,128)}) custom-call(f32[10,64,128]{2,1,0:T(8,128)S(1)} %get-tuple-element.6.state_ref, f32[10,64,128]{2,1,0:T(8,128)S(1)} %get-tuple-element.7.buddy_ref), custom_call_target="tpu_custom_call" | custom-call | tf_op jit(solution)/shard_map/written/pallas_call | solution.py:455
